TPU v7x, 256 devices: a whole 4x4x8 slice. The times are simulated.
256 devices in a mesh: expert: 32 (over x, z), tensor: 8 (over y, core).
Axes of the slice: x: 4, y: 4, z: 8, core: 2. Of those that a mesh axis runs over, the one named last changes fastest.
Arguments:
- tokens: bfloat16 [8192, 4096], P('expert'), may hold values from -6 to 6
- cotangent: bfloat16 [8192, 4096], P('expert'), may hold values from -1.5 to 1.5
- w_in: bfloat16 [4096, 65536], P(None, ('expert', 'tensor')), may hold values from -0.09375 to 0.09375
- w_out: bfloat16 [65536, 4096], P(('expert', 'tensor')), may hold values from -0.09375 to 0.09375
- router: bfloat16 [4096, 16], replicated, may hold values from -0.09375 to 0.09375
- chosen: int32 [16, 512], replicated, may hold values from 0 to 8191, as said below
Outputs:
- grad_tokens: bfloat16 [8192, 4096], P('expert', 'tensor')
- grad_in: bfloat16 [4096, 65536], P(None, ('expert', 'tensor'))
- grad_out: bfloat16 [65536, 4096], P(('expert', 'tensor'))
- grad_router: float32 [4096, 16], replicated
Inputs may be any that keep to these rules, and one draw needn't show every extreme that they name: Row e lists, in increasing order, 512 distinct tokens chosen by expert e; at most 32 of them lie among one device's 256 consecutive tokens, and in every row some device's tokens hold exactly 32 of them.
All inputs are finite; a program needn't handle non-finite values.
Results may differ from a plain program's by a relative error of at most 0.005.
Values may be sent and summed in bfloat16 or wider, within the bound.
A program may use at most 128 MiB of HBM per device.

v0:
```python
import jax
import jax.numpy as jnp
from jax import lax
from jax.sharding import PartitionSpec as P


def body(tokens, cotangent, w_in, w_out, router, chosen):
    tok_dev, features = tokens.shape
    n_expert = lax.axis_size("expert")
    bucket = 4 * tok_dev // n_expert
    capacity = chosen.shape[1]
    expert_total = router.shape[1]
    device_index = lax.axis_index("expert")
    expert = device_index // 2
    slot_range = jnp.arange(bucket, dtype=jnp.int32)
    first_token = device_index * tok_dev
    starts = jnp.sum((chosen < first_token).astype(jnp.int32), axis=1)
    run_ends = jnp.sum((chosen < first_token + tok_dev).astype(jnp.int32), axis=1)
    counts = run_ends - starts
    positions = jnp.minimum(starts[:, None] + slot_range[None, :], capacity - 1)
    picked = jnp.take_along_axis(chosen, positions, axis=1) - first_token
    filled = slot_range[None, :] < counts[:, None]
    local_rows = jnp.where(filled, picked, 0)
    owner_expert = jnp.arange(n_expert, dtype=jnp.int32) // 2
    send_rows = local_rows[owner_expert].reshape(-1)
    send_filled = filled[owner_expert].reshape(-1)

    def pack(source):
        gathered = jnp.where(send_filled[:, None], source[send_rows], jnp.zeros((), source.dtype))
        return gathered.reshape(n_expert, bucket, source.shape[1])

    got_x, got_y = (
        lax.all_to_all(pack(tokens), "expert", split_axis=0, concat_axis=0, tiled=True),
        lax.all_to_all(pack(cotangent), "expert", split_axis=0, concat_axis=0, tiled=True),
    )
    my_chosen = lax.dynamic_index_in_dim(chosen, expert, 0, keepdims=False)
    home_index = my_chosen // tok_dev
    bounds = jnp.arange(n_expert, dtype=jnp.int32) * tok_dev
    run_start = jnp.sum((my_chosen[None, :] < bounds[:, None]).astype(jnp.int32), axis=1)
    slot_index = home_index * bucket + jnp.arange(capacity, dtype=jnp.int32) - run_start[home_index]
    x_rows = got_x.reshape(-1, features)[slot_index]
    grad_rows = got_y.reshape(-1, features)[slot_index]
    r_col = lax.dynamic_slice_in_dim(router, expert, 1, 1)
    gate = jax.nn.sigmoid(jnp.dot(x_rows, r_col, preferred_element_type=jnp.float32)[:, 0])
    pre_act = jnp.dot(x_rows, w_in, preferred_element_type=jnp.float32)
    sig_act = jax.nn.sigmoid(pre_act)
    hidden = pre_act * sig_act
    upstream = jnp.dot(grad_rows, w_out.T, preferred_element_type=jnp.float32)
    gated_hidden = (gate[:, None] * hidden).astype(jnp.bfloat16)
    gate_grad = jnp.sum(hidden * upstream, axis=1)
    pre_grad = (gate[:, None] * upstream * sig_act * (1.0 + pre_act * (1.0 - sig_act))).astype(
        jnp.bfloat16
    )
    grad_out = jnp.dot(gated_hidden.T, grad_rows, preferred_element_type=jnp.float32).astype(
        jnp.bfloat16
    )
    grad_in = jnp.dot(x_rows.T, pre_grad, preferred_element_type=jnp.float32).astype(jnp.bfloat16)
    score_grad = gate_grad * gate * (1.0 - gate)
    router_col = jnp.dot(score_grad, x_rows.astype(jnp.float32), precision=lax.Precision.HIGHEST)
    router_term = (
        router_col[:, None] * (jnp.arange(expert_total) == expert).astype(jnp.float32)[None, :]
    )
    grad_router = lax.psum(router_term, ("expert", "tensor"))
    router_rows = r_col.astype(jnp.float32)
    summed = lax.psum_scatter(
        jnp.dot(w_in, pre_grad.T, preferred_element_type=jnp.float32)
        + router_rows * score_grad[None, :],
        "tensor",
        scatter_dimension=0,
        tiled=True,
    )
    share = summed.shape[0]
    outgoing = jnp.zeros((share, n_expert * bucket), jnp.float32).at[:, slot_index].set(summed)
    returned = lax.all_to_all(
        outgoing.reshape(share, n_expert, bucket), "expert", split_axis=1, concat_axis=1, tiled=True
    )
    returned = jnp.where(send_filled[None, :], returned.reshape(share, -1), 0.0)
    combined = jnp.zeros((share, tok_dev), jnp.float32).at[:, send_rows].add(returned)
    grad_tokens = combined.T.astype(jnp.bfloat16)
    return (grad_tokens, grad_in, grad_out, grad_router)


def solution(mesh):
    placed = (
        P("expert", None),
        P("expert", None),
        P(None, ("expert", "tensor")),
        P(("expert", "tensor"), None),
        P(),
        P(),
    )
    return jax.shard_map(
        body,
        mesh=mesh,
        in_specs=placed,
        out_specs=(
            P("expert", "tensor"),
            P(None, ("expert", "tensor")),
            P(("expert", "tensor"), None),
            P(),
        ),
        check_vma=False,
    )
```

profile of v0, /device:TPU:2, one launch (start us, length us, event | category | flops | bytes accessed | tf_op | source)
XLA Modules:
  0.0 806.7 jit_solution(2339139497223671526)
XLA Ops:
  8.1 1.0 convert_reduce_fusion.2
  9.1 0.1 fusion.13
  9.2 0.1 reshape.418
  9.2 4.5 gather_fusion.6
  13.8 0.1 reshape.421
  13.8 0.1 iota_compare_fusion
  13.9 0.1 subtract_select_fusion
  14.0 0.6 gather_fusion
  14.6 0.1 reshape.325
  14.7 0.6 gather_fusion.1
  15.3 7.8 gather_fusion.4
  23.1 16.9 %gather_fusion.2 = bf16[1024,4096]{1,0:T(8,128)(2,1)} fusion(bf16[256,4096]{1,0:T(8,128)(2,1)} %param.6, s32[1024]{0:T(1024)S(1)} %broadcast_clamp_fusion), kind=kCustom, calls=%fused_computation.2 | custom fusion | bytes 16781312 | tf_op jit(solution)/shard_map/gather | solution.py:29
  40.0 9.2 %broadcast_select_fusion = (bf16[32,32,4096]{2,1,0:T(8,128)(2,1)}, bf16[32,32,4096]{2,1,0:T(8,128)(2,1)S(1)}) fusion(bf16[32,32,4096]{2,1,0:T(8,128)(2,1)} %bitcast.83, pred[32,32]{1,0:T(8,128)(4,1)S(1)} %gather_fusion.1, bf16[32,32,4096]{2,1,0:T(8,128)(2,1)} %bitcast.84), kind=kLoop, calls=%fused_computation.10 | loop fusion | flops 8388608 | bytes 33555456 | tf_op jit(solution)/shard_map/jit(_where)/select_n | solution.py:29
  49.2 194.9 %all_to_all.15 = bf16[32,32,4096]{2,1,0:T(8,128)(2,1)} all-to-all(bf16[32,32,4096]{2,1,0:T(8,128)(2,1)S(1)} %get-tuple-element.37), channel_id=1, replica_groups=mesh['expert'=32,'tensor'=8] {'expert'}, dimensions={0} | all-to-all | bytes 16777216 | tf_op jit(solution)/shard_map/all_to_all | solution.py:33
  244.1 7.7 all-to-all-start.1
  251.8 0.0 reduce-scatter.2.cloned.1.call-start
  251.9 0.9 dynamic-slice_reduce_fusion
  252.8 0.2 convert_reduce_fusion
  253.0 0.7 fusion.21
  253.7 4.3 compare_select_fusion.5
  258.1 0.7 fusion.20
  258.8 0.2 compare_reduce_fusion.24
  258.9 15.5 %select_select_fusion = s32[512]{0:T(512)S(1)} fusion(pred[512]{0:T(512)(128)(4,1)S(1)} %get-tuple-element.30, pred[512]{0:T(512)(128)(4,1)S(1)} %get-tuple-element.29, pred[512]{0:T(512)(128)(4,1)S(1)} %get-tuple-element.28, pred[512]{0:T(512)(128)(4,1)S(1)} %get-tuple-element.27, pred[512]{0:T(512)(128)(4,1)S(1)} %get-tuple-element.26, ...), kind=kLoop, calls=%fused_computation.88 | loop fusion | flops 12800 | bytes 16996 | tf_op jit(solution)/shard_map/gather | solution.py:40
  274.5 13.3 %gather_fusion.3 = bf16[512,4096]{1,0:T(8,128)(2,1)} fusion(bf16[1024,4096]{1,0:T(8,128)(2,1)} %bitcast.82, s32[1024]{0:T(1024)S(1)} %pad_clamp_fusion), kind=kCustom, calls=%fused_computation.3 | custom fusion | bytes 8390656 | tf_op jit(solution)/shard_map/gather | solution.py:41
  287.9 3.5 fusion.9
  291.4 0.0 copy-done.5
  291.4 1.3 fusion.22
  292.7 144.1 %all-to-all-done.1 = bf16[32,32,4096]{2,1,0:T(8,128)(2,1)} async-done(((bf16[32,32,4096]{2,1,0:T(8,128)(2,1)}), bf16[32,32,4096]{2,1,0:T(8,128)(2,1)}, u32[]{:S(2)}, u32[]{:S(2)}) %all-to-all-start.1) | async-done | bytes 8388640 | tf_op jit(solution)/shard_map/all_to_all | solution.py:34
  436.9 13.0 %gather_fusion.5 = bf16[512,4096]{1,0:T(8,128)(2,1)} fusion(bf16[1024,4096]{1,0:T(8,128)(2,1)} %bitcast.43, s32[1024]{0:T(1024)S(1)} %pad_clamp_fusion), kind=kCustom, calls=%fused_computation.5 | custom fusion | bytes 8390656 | tf_op jit(solution)/shard_map/gather | solution.py:42
  449.9 4.3 multiply_reduce_fusion
  454.2 5.1 bitcast_add_fusion
  459.3 0.0 reduce-scatter.2.cloned.1.call-update
  459.3 57.6 %reduce-scatter.2.cloned.1.call-done = f32[512,512]{0,1:T(8,128)} async-done(((f32[4096,512]{0,1:T(8,128)}), f32[512,512]{0,1:T(8,128)}) %reduce-scatter.2.cloned.1.call-update) | async-done | bytes 1048592 | tf_op jit(solution)/shard_map/reduce_scatter | solution.py:65
  517.0 4.4 scatter_custom_fusion
  521.4 10.2 %all-to-all-start.2 = ((f32[512,32,32]{0,2,1:T(8,128)}), f32[512,32,32]{0,2,1:T(8,128)}, u32[]{:S(2)}, u32[]{:S(2)}) async-start(f32[512,32,32]{0,2,1:T(8,128)} %bitcast.46), calls=%async_computation.3 | async-start | bytes 4194304 | tf_op jit(solution)/shard_map/all_to_all | solution.py:74
  531.6 0.0 all-reduce.2.cloned.1.call-start
  531.6 0.1 broadcast_in_dim.36
  531.7 3.9 fusion.23
  535.6 0.8 broadcast_multiply_fusion
  536.4 0.0 all-reduce.2.cloned.1.call-update
  536.5 5.0 convolution_convert_fusion.1
  541.4 2.6 convolution_convert_fusion
  544.1 34.9 %all-to-all-done.2 = f32[512,32,32]{0,2,1:T(8,128)} async-done(((f32[512,32,32]{0,2,1:T(8,128)}), f32[512,32,32]{0,2,1:T(8,128)}, u32[]{:S(2)}, u32[]{:S(2)}) %all-to-all-start.2) | async-done | bytes 2097184 | tf_op jit(solution)/shard_map/all_to_all | solution.py:74
  579.0 3.2 bitcast_select_fusion
  582.2 7.6 scatter_custom_fusion.1
  589.8 0.7 convert_bitcast_fusion
  590.5 207.0 %all-reduce.2.cloned.1.call-done = f32[4096,16]{0,1:T(8,128)} async-done(((f32[4096,16]{0,1:T(8,128)}), f32[4096,16]{0,1:T(8,128)}) %all-reduce.2.cloned.1.call-update) | async-done | bytes 262160 | tf_op jit(solution)/shard_map/psum | solution.py:63
  797.6 1.7 copy.11
  (24 shorter events, 0.1 us)
Async XLA Ops:
  8.0 7.3 copy-start
  8.0 1.2 copy-start.2
  244.1 192.7 %all-to-all-start.1 = ((bf16[32,32,4096]{2,1,0:T(8,128)(2,1)}), bf16[32,32,4096]{2,1,0:T(8,128)(2,1)}, u32[]{:S(2)}, u32[]{:S(2)}) async-start(bf16[32,32,4096]{2,1,0:T(8,128)(2,1)} %get-tuple-element.36), calls=%async_computation.1 | async-start | bytes 16777216 | tf_op jit(solution)/shard_map/all_to_all | solution.py:34
  251.8 265.1 %reduce-scatter.2.cloned.1.call-start = ((), (), s32[]{:S(2)}) async-start(), calls=%async_computation.4 | async-start | bytes 9437184 | tf_op jit(solution)/shard_map/reduce_scatter | solution.py:65
  274.5 16.9 %copy-start.5 = (bf16[4096,256]{1,0:T(8,128)(2,1)S(1)}, bf16[4096,256]{1,0:T(8,128)(2,1)}, u32[]{:S(2)}) copy-start(bf16[4096,256]{1,0:T(8,128)(2,1)} %param.8) | copy-start | bytes 6291460
  287.9 3.5 copy-start.3
  521.4 57.6 %all-to-all-start.2 = ((f32[512,32,32]{0,2,1:T(8,128)}), f32[512,32,32]{0,2,1:T(8,128)}, u32[]{:S(2)}, u32[]{:S(2)}) async-start(f32[512,32,32]{0,2,1:T(8,128)} %bitcast.46), calls=%async_computation.3 | async-start | bytes 4194304 | tf_op jit(solution)/shard_map/all_to_all | solution.py:74
  531.6 266.0 %all-reduce.2.cloned.1.call-start = ((), (), s32[]{:S(2)}) async-start(), calls=%async_computation.5 | async-start | bytes 524288 | tf_op jit(solution)/shard_map/psum | solution.py:63
  536.5 5.0 copy-start.4
  541.4 257.8 %copy-start.1 = (bf16[256,4096]{1,0:T(8,128)(2,1)S(1)}, bf16[256,4096]{1,0:T(8,128)(2,1)}, u32[]{:S(2)}) copy-start(bf16[256,4096]{1,0:T(8,128)(2,1)} %param.7) | copy-start | bytes 6291460
Sparse Core Ops, SparseCore 0:
  459.4 57.4 reduce-scatter.1
Sparse Core Ops, SparseCore 1:
  538.1 259.4 all-reduce.1
where the time goes:
time: 808 us; the launch traced here: 807 us
  waiting for transfers between devices  444 us (55%)
  blocking collectives  195 us (24%)
  local copies, waits for them, and re-layouts  65.6 us (8%)
  other arithmetic  43 us (5%)
  matrix products  25.8 us (3%)
  starting transfers between devices  18 us (2%)
  between operations  15.7 us (2%)
    psum x1, waiting for transfers between devices, body(): grad_router = lax.psum(router_term, ('expert', 'tensor'))  207 us
    all_to_all x1, blocking collectives, body(): lax.all_to_all(pack(tokens), 'expert', split_axis=0, concat_axis=0, tiled...  195 us
    all_to_all x1, waiting for transfers between devices, body(): lax.all_to_all(pack(cotangent), 'expert', split_axis=0, concat_axis=0, ti...  144 us
    reduce_scatter x1, waiting for transfers between devices, body(): lax.psum_scatter(jnp.dot(w_in, pre_grad.T, preferred_element_type=jnp.flo...  57.6 us
    all_to_all x1, waiting for transfers between devices, body(): lax.all_to_all(outgoing.reshape(share, n_expert, bucket), 'expert', split...  34.9 us
    gather x2, local copies, waits for them, and re-layouts, pack(): source[send_rows]  24.8 us
    gather x3, other arithmetic, body(): run_start[home_index]  20 us
  transfers between devices with their start and end apart: 4, of which 4 were waited for; matrix products, arithmetic and copies ran while one was open for 8% of the time, Pallas kernels for 0%

commit v1 on v0

--- a/solution.py
+++ b/solution.py
@@ -60,7 +60,7 @@
     router_term = (
         router_col[:, None] * (jnp.arange(expert_total) == expert).astype(jnp.float32)[None, :]
     )
-    grad_router = lax.psum(router_term, ("expert", "tensor"))
+    grad_router = lax.psum(lax.psum(router_term, "expert"), "tensor")
     router_rows = r_col.astype(jnp.float32)
     summed = lax.psum_scatter(
         jnp.dot(w_in, pre_grad.T, preferred_element_type=jnp.float32)

time: 808 us -> 760 us (0.941)
  waiting for transfers between devices: 444 us -> 396 us
    all_to_all x1, waiting for transfers between devices: 34.9 us -> 0.01 us  [body(): lax.all_to_all(outgoing.reshape(share, n_expert, bucket), 'expert', split...]
    psum x1 -> x2, waiting for transfers between devices: 207 us -> 194 us  [body(): grad_router = lax.psum(lax.psum(router_term, 'expert'), 'tensor')]
  transfers between devices with their start and end apart: 4 -> 5, of which waited for: 4 -> 4; matrix products, arithmetic and copies ran while one was open for 8% -> 9% of each run, Pallas kernels for 0% -> 0%
where the time goes in v1:
time: 760 us; the launch traced here: 759 us
  waiting for transfers between devices  396 us (52%)
  blocking collectives  195 us (26%)
  local copies, waits for them, and re-layouts  65.6 us (9%)
  other arithmetic  43.2 us (6%)
  matrix products  25.7 us (3%)
  starting transfers between devices  18 us (2%)
  between operations  15.7 us (2%)
    all_to_all x1, blocking collectives, body(): lax.all_to_all(pack(tokens), 'expert', split_axis=0, concat_axis=0, tiled...  195 us
    psum x2, waiting for transfers between devices, body(): grad_router = lax.psum(lax.psum(router_term, 'expert'), 'tensor')  194 us
    all_to_all x1, waiting for transfers between devices, body(): lax.all_to_all(pack(cotangent), 'expert', split_axis=0, concat_axis=0, ti...  144 us
    reduce_scatter x1, waiting for transfers between devices, body(): lax.psum_scatter(jnp.dot(w_in, pre_grad.T, preferred_element_type=jnp.flo...  57.6 us
    gather x2, local copies, waits for them, and re-layouts, pack(): source[send_rows]  24.8 us
    gather x3, other arithmetic, body(): run_start[home_index]  20 us
  transfers between devices with their start and end apart: 5, of which 4 were waited for; matrix products, arithmetic and copies ran while one was open for 9% of the time, Pallas kernels for 0%

profile of v1, /device:TPU:2, one launch (start us, length us, event | category | flops | bytes accessed | tf_op | source)
XLA Modules:
  0.0 759.1 jit_solution(7239756265299898916)
XLA Ops:
  8.1 1.0 convert_reduce_fusion.2
  9.1 0.1 fusion.13
  9.2 0.1 reshape.418
  9.2 4.5 gather_fusion.6
  13.8 0.1 reshape.421
  13.8 0.1 iota_compare_fusion
  13.9 0.1 subtract_select_fusion
  14.0 0.6 gather_fusion
  14.6 0.1 reshape.325
  14.7 0.6 gather_fusion.1
  15.3 7.8 %gather_fusion.4 = bf16[1024,4096]{1,0:T(8,128)(2,1)} fusion(bf16[256,4096]{1,0:T(8,128)(2,1)S(1)} %copy-done, s32[1024]{0:T(1024)S(1)} %broadcast_clamp_fusion), kind=kCustom, calls=%fused_computation.4 | custom fusion | bytes 16781312 | tf_op jit(solution)/shard_map/gather | solution.py:29
  23.1 16.9 %gather_fusion.2 = bf16[1024,4096]{1,0:T(8,128)(2,1)} fusion(bf16[256,4096]{1,0:T(8,128)(2,1)} %param.6, s32[1024]{0:T(1024)S(1)} %broadcast_clamp_fusion), kind=kCustom, calls=%fused_computation.2 | custom fusion | bytes 16781312 | tf_op jit(solution)/shard_map/gather | solution.py:29
  40.0 9.2 %broadcast_select_fusion = (bf16[32,32,4096]{2,1,0:T(8,128)(2,1)}, bf16[32,32,4096]{2,1,0:T(8,128)(2,1)S(1)}) fusion(bf16[32,32,4096]{2,1,0:T(8,128)(2,1)} %bitcast.83, pred[32,32]{1,0:T(8,128)(4,1)S(1)} %gather_fusion.1, bf16[32,32,4096]{2,1,0:T(8,128)(2,1)} %bitcast.84), kind=kLoop, calls=%fused_computation.10 | loop fusion | flops 8388608 | bytes 33555456 | tf_op jit(solution)/shard_map/jit(_where)/select_n | solution.py:29
  49.2 194.9 %all_to_all.15 = bf16[32,32,4096]{2,1,0:T(8,128)(2,1)} all-to-all(bf16[32,32,4096]{2,1,0:T(8,128)(2,1)S(1)} %get-tuple-element.37), channel_id=1, replica_groups=mesh['expert'=32,'tensor'=8] {'expert'}, dimensions={0} | all-to-all | bytes 16777216 | tf_op jit(solution)/shard_map/all_to_all | solution.py:33
  244.1 7.7 %all-to-all-start.1 = ((bf16[32,32,4096]{2,1,0:T(8,128)(2,1)}), bf16[32,32,4096]{2,1,0:T(8,128)(2,1)}, u32[]{:S(2)}, u32[]{:S(2)}) async-start(bf16[32,32,4096]{2,1,0:T(8,128)(2,1)} %get-tuple-element.36), calls=%async_computation.1 | async-start | bytes 16777216 | tf_op jit(solution)/shard_map/all_to_all | solution.py:34
  251.8 0.0 reduce-scatter.2.cloned.1.call-start
  251.9 0.9 dynamic-slice_reduce_fusion
  252.8 0.2 convert_reduce_fusion
  253.0 0.7 fusion.21
  253.7 4.3 compare_select_fusion.5
  258.1 0.7 fusion.20
  258.8 0.2 compare_reduce_fusion.24
  258.9 15.5 %select_select_fusion = s32[512]{0:T(512)S(1)} fusion(pred[512]{0:T(512)(128)(4,1)S(1)} %get-tuple-element.30, pred[512]{0:T(512)(128)(4,1)S(1)} %get-tuple-element.29, pred[512]{0:T(512)(128)(4,1)S(1)} %get-tuple-element.28, pred[512]{0:T(512)(128)(4,1)S(1)} %get-tuple-element.27, pred[512]{0:T(512)(128)(4,1)S(1)} %get-tuple-element.26, ...), kind=kLoop, calls=%fused_computation.88 | loop fusion | flops 12800 | bytes 16996 | tf_op jit(solution)/shard_map/gather | solution.py:40
  274.5 13.3 %gather_fusion.3 = bf16[512,4096]{1,0:T(8,128)(2,1)} fusion(bf16[1024,4096]{1,0:T(8,128)(2,1)} %bitcast.82, s32[1024]{0:T(1024)S(1)} %pad_clamp_fusion), kind=kCustom, calls=%fused_computation.3 | custom fusion | bytes 8390656 | tf_op jit(solution)/shard_map/gather | solution.py:41
  287.9 3.5 fusion.9
  291.4 1.3 fusion.22
  292.7 144.1 %all-to-all-done.1 = bf16[32,32,4096]{2,1,0:T(8,128)(2,1)} async-done(((bf16[32,32,4096]{2,1,0:T(8,128)(2,1)}), bf16[32,32,4096]{2,1,0:T(8,128)(2,1)}, u32[]{:S(2)}, u32[]{:S(2)}) %all-to-all-start.1) | async-done | bytes 8388640 | tf_op jit(solution)/shard_map/all_to_all | solution.py:34
  436.9 13.0 %gather_fusion.5 = bf16[512,4096]{1,0:T(8,128)(2,1)} fusion(bf16[1024,4096]{1,0:T(8,128)(2,1)} %bitcast.43, s32[1024]{0:T(1024)S(1)} %pad_clamp_fusion), kind=kCustom, calls=%fused_computation.5 | custom fusion | bytes 8390656 | tf_op jit(solution)/shard_map/gather | solution.py:42
  449.9 4.3 multiply_reduce_fusion
  454.2 5.1 bitcast_add_fusion
  459.3 0.0 reduce-scatter.2.cloned.1.call-update
  459.3 57.6 %reduce-scatter.2.cloned.1.call-done = f32[512,512]{0,1:T(8,128)} async-done(((f32[4096,512]{0,1:T(8,128)}), f32[512,512]{0,1:T(8,128)}) %reduce-scatter.2.cloned.1.call-update) | async-done | bytes 1048592 | tf_op jit(solution)/shard_map/reduce_scatter | solution.py:65
  517.0 4.4 scatter_custom_fusion
  521.4 10.2 %all-to-all-start.2 = ((f32[512,32,32]{0,2,1:T(8,128)}), f32[512,32,32]{0,2,1:T(8,128)}, u32[]{:S(2)}, u32[]{:S(2)}) async-start(f32[512,32,32]{0,2,1:T(8,128)} %bitcast.46), calls=%async_computation.3 | async-start | bytes 4194304 | tf_op jit(solution)/shard_map/all_to_all | solution.py:74
  531.6 0.0 all-reduce.3.cloned.1.call-start
  531.6 0.1 broadcast_in_dim.36
  531.7 3.9 fusion.23
  535.6 0.8 broadcast_multiply_fusion
  536.4 0.0 all-reduce.3.cloned.1.call-update
  536.5 0.0 all-reduce.5.cloned.1.call-start
  536.5 4.9 convolution_convert_fusion
  541.5 2.6 convolution_convert_fusion.1
  544.1 142.0 %all-reduce.3.cloned.1.call-done = f32[4096,16]{0,1:T(8,128)} async-done(((f32[4096,16]{0,1:T(8,128)}), f32[4096,16]{0,1:T(8,128)}) %all-reduce.3.cloned.1.call-update) | async-done | bytes 262160 | tf_op jit(solution)/shard_map/psum | solution.py:63
  686.1 3.3 bitcast_select_fusion
  689.4 7.6 %scatter_custom_fusion.1 = f32[512,256]{0,1:T(8,128)S(1)} fusion(s32[1024]{0:T(1024)S(1)} %bitcast.90, f32[512,1024]{0,1:T(8,128)} %bitcast_select_fusion, f32[]{:T(128)} %constant.70.clone.1), kind=kCustom, calls=%fused_computation.14 | custom fusion | flops 524288 | bytes 2621444 | tf_op jit(solution)/shard_map/scatter-add | solution.py:78
  697.1 0.7 convert_bitcast_fusion
  697.8 52.2 %all-reduce.5.cloned.1.call-done = f32[4096,16]{0,1:T(8,128)} async-done(((f32[4096,16]{0,1:T(8,128)}), f32[4096,16]{0,1:T(8,128)}) %all-reduce.5.cloned.1.call-update) | async-done | bytes 262160 | tf_op jit(solution)/shard_map/psum | solution.py:63
  750.0 1.7 copy.12
  (27 shorter events, 0.2 us)
Async XLA Ops:
  8.0 7.3 copy-start
  8.0 1.2 copy-start.2
  244.1 192.7 %all-to-all-start.1 = ((bf16[32,32,4096]{2,1,0:T(8,128)(2,1)}), bf16[32,32,4096]{2,1,0:T(8,128)(2,1)}, u32[]{:S(2)}, u32[]{:S(2)}) async-start(bf16[32,32,4096]{2,1,0:T(8,128)(2,1)} %get-tuple-element.36), calls=%async_computation.1 | async-start | bytes 16777216 | tf_op jit(solution)/shard_map/all_to_all | solution.py:34
  251.8 265.1 %reduce-scatter.2.cloned.1.call-start = ((), (), s32[]{:S(2)}) async-start(), calls=%async_computation.4 | async-start | bytes 9437184 | tf_op jit(solution)/shard_map/reduce_scatter | solution.py:65
  274.5 16.9 %copy-start.5 = (bf16[4096,256]{1,0:T(8,128)(2,1)S(1)}, bf16[4096,256]{1,0:T(8,128)(2,1)}, u32[]{:S(2)}) copy-start(bf16[4096,256]{1,0:T(8,128)(2,1)} %param.8) | copy-start | bytes 6291460
  287.9 3.5 copy-start.3
  521.4 164.7 %all-to-all-start.2 = ((f32[512,32,32]{0,2,1:T(8,128)}), f32[512,32,32]{0,2,1:T(8,128)}, u32[]{:S(2)}, u32[]{:S(2)}) async-start(f32[512,32,32]{0,2,1:T(8,128)} %bitcast.46), calls=%async_computation.3 | async-start | bytes 4194304 | tf_op jit(solution)/shard_map/all_to_all | solution.py:74
  531.6 154.5 %all-reduce.3.cloned.1.call-start = ((), (), s32[]{:S(2)}) async-start(), calls=%async_computation.5 | async-start | bytes 524288 | tf_op jit(solution)/shard_map/psum | solution.py:63
  536.5 213.6 %all-reduce.5.cloned.1.call-start = ((), (), s32[]{:S(2)}) async-start(), calls=%async_computation.6 | async-start | bytes 524288 | tf_op jit(solution)/shard_map/psum | solution.py:63
  536.5 5.0 copy-start.4
  686.1 65.6 %copy-start.1 = (bf16[256,4096]{1,0:T(8,128)(2,1)S(1)}, bf16[256,4096]{1,0:T(8,128)(2,1)}, u32[]{:S(2)}) copy-start(bf16[256,4096]{1,0:T(8,128)(2,1)} %param.7) | copy-start | bytes 6291460
Sparse Core Ops, SparseCore 0:
  459.4 57.4 reduce-scatter.1
  686.2 63.7 all-reduce.4
Sparse Core Ops, SparseCore 1:
  536.5 149.5 all-reduce.2
